TPU v7x, 1024 devices: a whole 4x4x32 slice. The times are simulated.
1024 devices in a mesh: dp: 16 (over x_lo, y, core), seq: 64 (over z, x_hi).
Axes of the slice: x: 4 (x_hi: 2, x_lo: 2; x = x_hi * 2 + x_lo), y: 4, z: 32, core: 2. Of those that a mesh axis runs over, the one named last changes fastest.
Arguments:
- tokens: bfloat16 [131072, 1024], P(('dp', 'seq')), may hold values from -6 to 6
- gate_values: float32 [131072, 2], P(('dp', 'seq')), may hold values from 0.2 to 1
- expert_ids: int32 [131072, 2], P(('dp', 'seq')), may hold values from 0 to 31, all different within a row; in each aligned block of 128 rows (0 to 127, 128 to 255, ...) at most 9 rows name the same one
- cotangent: bfloat16 [131072, 1024], P(('dp', 'seq')), may hold values from -6 to 6
- weight_in: bfloat16 [32768, 1024], P('seq'), may hold values from -0.1875 to 0.1875
- weight_out: bfloat16 [32768, 1024], P('seq'), may hold values from -0.1875 to 0.1875
Outputs:
- layer_out: bfloat16 [131072, 1024], P(('dp', 'seq'))
- gate_grad: float32 [131072, 2], P(('dp', 'seq'))
- input_grad: bfloat16 [131072, 1024], P(('dp', 'seq'))
- weight_in_grad: float32 [1024, 32768], P('dp', 'seq')
- weight_out_grad: float32 [1024, 32768], P('dp', 'seq')
Inputs may be any that keep to these rules, and one draw needn't show every extreme that they name: `expert_ids`: each row names two different experts; within the rows of one device no expert is named more than 9 times, a bound that some block reaches.
All inputs are finite; a program needn't handle non-finite values.
Results may differ from a plain program's by a relative error of at most 0.017.
Values may be sent and summed in bfloat16 or wider, within the bound.
A program may use at most 64 MiB of HBM per device.

v0:
```python
import jax
import jax.numpy as jnp
import numpy as np
from jax import lax
from jax.sharding import PartitionSpec as P

E = 32
FF = 1024
CAP = 9


gelu_scale = 0.7978845608028654
gelu_cubic = 0.044715


def gelu_value(values):
    inner_arg = gelu_scale * (values + gelu_cubic * values * values * values)
    return 0.5 * values * (1.0 + jnp.tanh(inner_arg))


def gelu_slope(values):
    inner_arg = gelu_scale * (values + gelu_cubic * values * values * values)
    tanh_val = jnp.tanh(inner_arg)
    return 0.5 * (1.0 + tanh_val) + 0.5 * values * (1.0 - tanh_val * tanh_val) * gelu_scale * (
        1.0 + 3.0 * gelu_cubic * values * values
    )


def slot_numbers(ids_block):
    flat_ids = ids_block.reshape(-1)
    onehot = (flat_ids[:, None] == jnp.arange(E, dtype=jnp.int32)[None, :]).astype(jnp.int32)
    before = jnp.cumsum(onehot, axis=0) - onehot
    return jnp.sum(before * onehot, axis=1).reshape(ids_block.shape)


def local(tokens, gate_values, expert_ids, cotangent, weight_in, weight_out):
    seq_count = lax.axis_size("seq")
    group_count = lax.axis_size("dp")
    own_units = weight_in.shape[0]
    block_units = min(FF, own_units)
    held_experts = own_units // block_units
    block_count = FF // block_units
    tok_count = tokens.shape[0]
    model_width = tokens.shape[1]
    factor = (E / (2.0 * tok_count * seq_count * group_count)) ** 0.5
    row_total = seq_count * CAP
    slot_of = slot_numbers(expert_ids)
    flat_target = (expert_ids * CAP + slot_of).reshape(-1)
    token_of = jnp.repeat(jnp.arange(tok_count, dtype=jnp.int32), 2)
    slot_token = jnp.zeros((E * CAP,), jnp.int32).at[flat_target].set(token_of)
    slot_used = jnp.zeros((E * CAP,), jnp.float32).at[flat_target].set(1.0)
    slot_gate = jnp.zeros((E * CAP,), jnp.float32).at[flat_target].set(gate_values.reshape(-1))
    column = np.arange(seq_count * held_experts * CAP)
    owner_of = column // (held_experts * CAP)
    local_of = column // CAP % held_experts
    expert_of = (owner_of * own_units + local_of * block_units) // FF
    code_table = jnp.asarray(expert_of * CAP + column % CAP, dtype=jnp.int32)
    col_token = slot_token[code_table]
    col_used = slot_used[code_table]
    col_gate = slot_gate[code_table]
    send_shape = (seq_count, held_experts * CAP, model_width)
    send_x = (
        (tokens[col_token].astype(jnp.float32) * col_used[:, None])
        .astype(jnp.bfloat16)
        .reshape(send_shape)
    )
    send_d = (
        (cotangent[col_token].astype(jnp.float32) * col_gate[:, None])
        .astype(jnp.bfloat16)
        .reshape(send_shape)
    )
    win_local = weight_in.reshape(held_experts, block_units, model_width)
    wout_local = weight_out.reshape(held_experts, block_units, model_width)

    def to_rows(arrived):
        grouped = arrived.reshape(seq_count, held_experts, CAP, model_width)
        return jnp.transpose(grouped, (1, 0, 2, 3)).reshape(held_experts, row_total, model_width)

    def from_rows(results):
        grouped = results.reshape(held_experts, seq_count, CAP, model_width)
        return jnp.transpose(grouped, (1, 0, 2, 3)).reshape(send_shape)

    rows_x = to_rows(lax.all_to_all(send_x, "seq", split_axis=0, concat_axis=0, tiled=True))
    hidden = jnp.einsum("krd,kfd->krf", rows_x, win_local, preferred_element_type=jnp.float32)
    owner_act = gelu_value(hidden).astype(jnp.bfloat16)
    part_out = jnp.einsum(
        "krf,kfd->krd", owner_act, wout_local, preferred_element_type=jnp.float32
    ).astype(jnp.bfloat16)
    hidden, act, part_out = (hidden, owner_act, part_out)
    back_out = lax.all_to_all(from_rows(part_out), "seq", split_axis=0, concat_axis=0, tiled=True)
    rows_d = to_rows(lax.all_to_all(send_d, "seq", split_axis=0, concat_axis=0, tiled=True))
    back_hidden = jnp.einsum("krd,kfd->krf", rows_d, wout_local, preferred_element_type=jnp.float32)
    owner_dhid = (back_hidden * gelu_slope(hidden)).astype(jnp.bfloat16)
    part_in = jnp.einsum(
        "krf,kfd->krd", owner_dhid, win_local, preferred_element_type=jnp.float32
    ).astype(jnp.bfloat16)
    dhid, part_in = (owner_dhid, part_in)
    back_in = lax.all_to_all(from_rows(part_in), "seq", split_axis=0, concat_axis=0, tiled=True)

    def collect(returned):
        flat_rows = returned.reshape(-1, model_width)
        summed = jnp.zeros((tok_count, 2, model_width), jnp.float32)
        for block_index in range(block_count):
            unit_start = expert_ids * FF + block_index * block_units
            row_at = (
                unit_start // own_units * (held_experts * CAP)
                + unit_start % own_units // block_units * CAP
                + slot_of
            )
            summed = summed + flat_rows[row_at].astype(jnp.float32)
        return summed

    expert_out = collect(back_out)
    layer_out = jnp.sum(gate_values[:, :, None] * expert_out, axis=1).astype(jnp.bfloat16)
    gate_grad = jnp.sum(cotangent.astype(jnp.float32)[:, None, :] * expert_out, axis=2)
    input_grad = jnp.sum(collect(back_in), axis=1).astype(jnp.bfloat16)
    x_columns = jnp.transpose(rows_x, (2, 0, 1))
    d_columns = jnp.transpose(rows_d, (2, 0, 1))
    grad_in_part = (
        jnp.einsum("dkr,krf->dkf", x_columns, dhid, preferred_element_type=jnp.float32).reshape(
            lax.axis_size("dp") * (model_width // group_count), own_units
        )
        * factor
    )
    grad_out_part = (
        jnp.einsum("dkr,krf->dkf", d_columns, act, preferred_element_type=jnp.float32).reshape(
            lax.axis_size("dp") * (model_width // group_count), own_units
        )
        * factor
    )
    summed_grads = lax.psum_scatter(
        jnp.concatenate([grad_in_part, grad_out_part], axis=1).astype(jnp.bfloat16),
        "dp",
        scatter_dimension=0,
        tiled=True,
    ).astype(jnp.float32)
    weight_in_grad = summed_grads[:, :own_units]
    weight_out_grad = summed_grads[:, own_units:]
    return (layer_out, gate_grad, input_grad, weight_in_grad, weight_out_grad)


def solution(mesh):
    in_specs = (
        P(("dp", "seq"), None),
        P(("dp", "seq"), None),
        P(("dp", "seq"), None),
        P(("dp", "seq"), None),
        P("seq", None),
        P("seq", None),
    )
    out_specs = (
        P(("dp", "seq"), None),
        P(("dp", "seq"), None),
        P(("dp", "seq"), None),
        P("dp", "seq"),
        P("dp", "seq"),
    )
    return jax.shard_map(local, mesh=mesh, in_specs=in_specs, out_specs=out_specs, check_vma=False)
```

profile of v0, /device:TPU:24, one launch (start us, length us, event | category | flops | bytes accessed | tf_op | source)
XLA Modules:
  0.0 902.0 jit_solution(15898376332119579705)
XLA Ops:
  13.3 4.0 gather_fusion.2
  19.0 4.0 gather_fusion
  23.0 2.9 gather_fusion.1
  25.9 2.1 reshape.197
  28.0 3.8 multiply_convert_fusion.1
  31.8 31.9 %all-to-all-start = ((bf16[64,9,1024]{2,1,0:T(8,128)(2,1)}), bf16[64,9,1024]{2,1,0:T(8,128)(2,1)S(1)}, u32[]{:S(2)}, u32[]{:S(2)}) async-start(bf16[64,9,1024]{2,1,0:T(8,128)(2,1)} %multiply_convert_fusion.1), calls=%async_computation | async-start | bytes 4194304 | tf_op jit(solution)/shard_map/all_to_all | solution.py:83
  65.5 4.0 gather_fusion.6
  70.2 3.4 gather_fusion.5
  73.6 3.4 reshape.198
  77.0 3.8 multiply_convert_fusion
  80.8 182.7 %all-to-all-done = bf16[64,9,1024]{2,1,0:T(8,128)(2,1)S(1)} async-done(((bf16[64,9,1024]{2,1,0:T(8,128)(2,1)}), bf16[64,9,1024]{2,1,0:T(8,128)(2,1)S(1)}, u32[]{:S(2)}, u32[]{:S(2)}) %all-to-all-start) | async-done | bytes 1179680 | tf_op jit(solution)/shard_map/all_to_all | solution.py:83
  263.5 5.8 all-to-all-start.2
  270.6 2.4 fusion.36
  276.1 3.3 reshape_transpose_reshape.12
  279.4 189.4 %all-to-all-done.2 = bf16[64,9,1024]{2,1,0:T(8,128)(2,1)} async-done(((bf16[64,9,1024]{2,1,0:T(8,128)(2,1)}), bf16[64,9,1024]{2,1,0:T(8,128)(2,1)}, u32[]{:S(2)}, u32[]{:S(2)}) %all-to-all-start.2) | async-done | bytes 1179680 | tf_op jit(solution)/shard_map/all_to_all | solution.py:91
  468.8 5.6 all-to-all-start.1
  474.4 3.6 reshape.193
  478.0 3.0 fusion.2
  483.7 3.3 reshape_transpose_reshape.13
  487.0 187.2 %all-to-all-done.1 = bf16[64,9,1024]{2,1,0:T(8,128)(2,1)} async-done(((bf16[64,9,1024]{2,1,0:T(8,128)(2,1)}), bf16[64,9,1024]{2,1,0:T(8,128)(2,1)}, u32[]{:S(2)}, u32[]{:S(2)}) %all-to-all-start.1) | async-done | bytes 1179680 | tf_op jit(solution)/shard_map/all_to_all | solution.py:90
  674.2 5.6 all-to-all-start.3
  681.4 2.6 reshape_transpose_reshape.15
  684.1 2.4 fusion
  687.7 2.6 copy.36
  691.6 78.5 %reduce-scatter.4.cloned.1.call-done = bf16[64,1024]{1,0:T(8,128)(2,1)} async-done(((bf16[1024,1024]{1,0:T(8,128)(2,1)}), bf16[64,1024]{1,0:T(8,128)(2,1)}) %reduce-scatter.4.cloned.1.call-update) | async-done | bytes 131088
  772.8 2.5 reshape.191
  777.7 101.8 %all-to-all-done.3 = bf16[64,9,1024]{2,1,0:T(8,128)(2,1)} async-done(((bf16[64,9,1024]{2,1,0:T(8,128)(2,1)}), bf16[64,9,1024]{2,1,0:T(8,128)(2,1)}, u32[]{:S(2)}, u32[]{:S(2)}) %all-to-all-start.3) | async-done | bytes 1179680 | tf_op jit(solution)/shard_map/all_to_all | solution.py:98
  879.5 2.5 reshape.194
  882.1 2.0 gather_fusion.8
  884.0 2.0 gather_fusion.7
  886.8 3.6 multiply_reduce_fusion
  893.1 2.1 reduce_sum.39
  (72 shorter events, 29.7 us)
Async XLA Ops:
  7.2 267.0 %copy-start = (bf16[512,1024]{1,0:T(8,128)(2,1)S(1)}, bf16[512,1024]{1,0:T(8,128)(2,1)}, u32[]{:S(2)}) copy-start(bf16[512,1024]{1,0:T(8,128)(2,1)} %param.12) | copy-start | bytes 3145732
  19.0 4.0 copy-start.2
  31.8 32.0 %copy-start.4 = (f32[128,2]{0,1:T(2,128)S(1)}, f32[128,2]{0,1:T(2,128)}, u32[]{:S(2)}) copy-start(f32[128,2]{0,1:T(2,128)} %param.8) | copy-start | bytes 3076
  31.8 231.7 %all-to-all-start = ((bf16[64,9,1024]{2,1,0:T(8,128)(2,1)}), bf16[64,9,1024]{2,1,0:T(8,128)(2,1)S(1)}, u32[]{:S(2)}, u32[]{:S(2)}) async-start(bf16[64,9,1024]{2,1,0:T(8,128)(2,1)} %multiply_convert_fusion.1), calls=%async_computation | async-start | bytes 4194304 | tf_op jit(solution)/shard_map/all_to_all | solution.py:83
  65.4 4.7 copy-start.1
  263.5 205.3 %all-to-all-start.2 = ((bf16[64,9,1024]{2,1,0:T(8,128)(2,1)}), bf16[64,9,1024]{2,1,0:T(8,128)(2,1)}, u32[]{:S(2)}, u32[]{:S(2)}) async-start(bf16[64,9,1024]{2,1,0:T(8,128)(2,1)} %multiply_convert_fusion), calls=%async_computation.2 | async-start | bytes 4194304 | tf_op jit(solution)/shard_map/all_to_all | solution.py:91
  273.0 1.1 copy-start.6
  468.8 205.3 %all-to-all-start.1 = ((bf16[64,9,1024]{2,1,0:T(8,128)(2,1)}), bf16[64,9,1024]{2,1,0:T(8,128)(2,1)}, u32[]{:S(2)}, u32[]{:S(2)}) async-start(bf16[64,9,1024]{2,1,0:T(8,128)(2,1)} %reshape_transpose_reshape.12), calls=%async_computation.1 | async-start | bytes 4194304 | tf_op jit(solution)/shard_map/all_to_all | solution.py:90
  478.0 3.9 copy-start.5
  481.1 0.8 copy-start.8
  674.2 205.3 %all-to-all-start.3 = ((bf16[64,9,1024]{2,1,0:T(8,128)(2,1)}), bf16[64,9,1024]{2,1,0:T(8,128)(2,1)}, u32[]{:S(2)}, u32[]{:S(2)}) async-start(bf16[64,9,1024]{2,1,0:T(8,128)(2,1)} %reshape_transpose_reshape.13), calls=%async_computation.3 | async-start | bytes 4194304 | tf_op jit(solution)/shard_map/all_to_all | solution.py:98
  679.8 90.3 %reduce-scatter.4.cloned.1.call-start = ((), (), s32[]{:S(2)}) async-start(), calls=%async_computation.5 | async-start | bytes 2228224
  681.4 2.6 copy-start.9
  684.0 2.4 copy-start.7
  690.3 0.9 copy-start.3
Sparse Core Ops, SparseCore 0:
  690.5 79.5 reduce-scatter.3
where the time goes:
time: 903 us; the launch traced here: 902 us
  waiting for transfers between devices  740 us (82%)
  local copies, waits for them, and re-layouts  67.3 us (7%)
  starting transfers between devices  49 us (5%)
  other arithmetic  19 us (2%)
  between operations  14.4 us (2%)
  matrix products  12.6 us (1%)
    all_to_all x1, waiting for transfers between devices, local(): lax.all_to_all(send_d, 'seq', split_axis=0, concat_axis=0, tiled=True)  189 us
    all_to_all x1, waiting for transfers between devices, local(): lax.all_to_all(from_rows(part_out), 'seq', split_axis=0, concat_axis=0, t...  187 us
    all_to_all x1, waiting for transfers between devices, local(): lax.all_to_all(send_x, 'seq', split_axis=0, concat_axis=0, tiled=True)  183 us
    all_to_all x1, waiting for transfers between devices, local(): lax.all_to_all(from_rows(part_in), 'seq', split_axis=0, concat_axis=0, ti...  102 us
    unnamed x2, waiting for transfers between devices  78.6 us
    all_to_all x1, starting transfers between devices, local(): lax.all_to_all(send_x, 'seq', split_axis=0, concat_axis=0, tiled=True)  31.9 us
  transfers between devices with their start and end apart: 5, of which 5 were waited for; matrix products, arithmetic and copies ran while one was open for 6% of the time, Pallas kernels for 0%

commit v1 on v0

v1 whole, which is shorter than its diff:
```python
import functools

import jax
import jax.numpy as jnp
from jax import lax
from jax.experimental import pallas as pl
from jax.experimental.pallas import tpu as pltpu
from jax.sharding import PartitionSpec as P

MESH = pl.DeviceIdType.MESH
BF16 = jnp.bfloat16
F32 = jnp.float32

D = 1024
E = 32
FF = 1024
CAP = 9
TOK = 128
ROWS = E * CAP
PLANES = 32
SLAB = 32
FCHUNK = 256

gelu_scale = 0.7978845608028654
gelu_cubic = 0.044715

VMEM = pl.BlockSpec(memory_space=pltpu.VMEM)


def plane_device(expert, plane):
    return {
        "dp": (expert % 8) // 4 * 8 + expert % 4 * 2 + expert // 16,
        "seq": plane * 2 + (expert % 16) // 8,
    }


def position():
    seq = lax.axis_index("seq")
    dp = lax.axis_index("dp")
    plane = seq // 2
    x_hi = seq % 2
    own = x_hi * 8 + dp // 8 * 4 + (dp // 2) % 4 + 16 * (dp % 2)
    return plane, x_hi, dp, own


def up_of(plane, x_hi):
    return {"seq": (plane + 1) % PLANES * 2 + x_hi}


def down_of(plane, x_hi):
    return {"seq": (plane + PLANES - 1) % PLANES * 2 + x_hi}


def enter(plane, x_hi, own):
    barrier = pltpu.get_barrier_semaphore()
    pl.semaphore_signal(barrier, inc=1, device_id=up_of(plane, x_hi), device_id_type=MESH)
    pl.semaphore_signal(barrier, inc=1, device_id=down_of(plane, x_hi), device_id_type=MESH)

    @pl.loop(1, E)
    def _(k):
        pl.semaphore_signal(
            barrier, inc=1, device_id=plane_device((own + k) % E, plane), device_id_type=MESH
        )

    pl.semaphore_wait(barrier, E + 1)


def dot_t(a, b):
    return lax.dot_general(a, b, (((1,), (1,)), ((), ())), preferred_element_type=F32)


def dot_cols(a, b):
    return lax.dot_general(a, b, (((0,), (0,)), ((), ())), preferred_element_type=F32)


def pick_kernel(ids_ref, gate_ref, tok_ref, cot_ref, send_ref, pos_ref):
    expert = lax.broadcasted_iota(jnp.int32, (E, TOK), 0)
    hot = [(expert == ids_ref[k : k + 1, :]).astype(F32) for k in range(2)]
    row = lax.broadcasted_iota(jnp.int32, (TOK, TOK), 0)
    col = lax.broadcasted_iota(jnp.int32, (TOK, TOK), 1)
    earlier = (row < col).astype(BF16)
    before = jnp.dot((hot[0] + hot[1]).astype(BF16), earlier, preferred_element_type=F32)
    slot_row = lax.broadcasted_iota(jnp.int32, (ROWS, TOK), 0)
    picks = []
    gates = jnp.zeros((ROWS, 1), F32)
    for k in range(2):
        slot = jnp.sum(before * hot[k], axis=0, keepdims=True).astype(jnp.int32)
        at = ids_ref[k : k + 1, :] * CAP + slot
        pos_ref[k : k + 1, :] = at
        pick = slot_row == at
        picks.append(pick)
        gates = gates + jnp.sum(
            jnp.where(pick, gate_ref[k : k + 1, :], 0.0), axis=1, keepdims=True
        )
    both = (picks[0] | picks[1]).astype(F32).astype(BF16)
    x_rows = jnp.dot(both, tok_ref[...], preferred_element_type=F32).astype(BF16)
    send_ref[:, 0:CAP] = x_rows.reshape(ROWS, 8, 128).reshape(E, CAP, 8, 128)
    d_rows = (jnp.dot(both, cot_ref[...], preferred_element_type=F32) * gates).astype(BF16)
    send_ref[:, CAP : 2 * CAP] = d_rows.reshape(ROWS, 8, 128).reshape(E, CAP, 8, 128)


def start_rows(plane, own, src, dst, ssem, rsem):
    keep = pltpu.make_async_copy(src.at[own], dst.at[own], ssem.at[0])
    keep.start()

    def copy(k):
        to = (own + k) % E
        return pltpu.make_async_remote_copy(
            src_ref=src.at[to],
            dst_ref=dst.at[own],
            send_sem=ssem.at[k],
            recv_sem=rsem.at[k],
            device_id=plane_device(to, plane),
            device_id_type=MESH,
        )

    @pl.loop(1, E)
    def _(k):
        copy(k).start()

    def finish():
        keep.wait()

        @pl.loop(1, E)
        def _(k):
            copy(k).wait()

    return finish


def gather_kernel(
    send_ref, win_ref, wout_ref, rows_ref, fin_ref, fout_ref,
    held, own_sem, tok_send, tok_recv, ring_send, ring_recv, host_send, host_recv,
):
    plane, x_hi, dp, own = position()
    up, down = up_of(plane, x_hi), down_of(plane, x_hi)
    slab = pl.ds(pl.multiple_of(dp * SLAB, SLAB), SLAB)
    place = pl.ds(pl.multiple_of(x_hi * (FF // 2) + dp * SLAB, SLAB), SLAB)
    locals_ = [
        pltpu.make_async_copy(ref.at[slab], held.at[a, plane], own_sem.at[a])
        for a, ref in enumerate((win_ref, wout_ref))
    ]
    for c in locals_:
        c.start()
    enter(plane, x_hi, own)
    for c in locals_:
        c.wait()
    full = (fin_ref, fout_ref)

    def ring(direction, a, step):
        if direction == 0:
            e, to = (plane - (step - 1) + 2 * PLANES) % PLANES, up
        else:
            e, to = (plane + (step - 1)) % PLANES, down
        return pltpu.make_async_remote_copy(
            src_ref=held.at[a, e],
            dst_ref=held.at[a, e],
            send_sem=ring_send.at[direction, a, step],
            recv_sem=ring_recv.at[direction, a, step],
            device_id=to,
            device_id_type=MESH,
        )

    def arrival(direction, a, step):
        e = (plane - step + 2 * PLANES) % PLANES if direction == 0 else (plane + step) % PLANES
        to = up if direction == 0 else down
        return pltpu.make_async_remote_copy(
            src_ref=held.at[a, e],
            dst_ref=held.at[a, e],
            send_sem=ring_send.at[direction, a, step],
            recv_sem=ring_recv.at[direction, a, step],
            device_id=to,
            device_id_type=MESH,
        )

    def to_host(a, e):
        return pltpu.make_async_remote_copy(
            src_ref=held.at[a, e],
            dst_ref=full[a].at[place],
            send_sem=host_send.at[a, e],
            recv_sem=host_recv.at[a, own],
            device_id=plane_device(e, plane),
            device_id_type=MESH,
        )

    def to_self(a, e):
        return pltpu.make_async_copy(held.at[a, e], full[a].at[place], host_recv.at[a, own])

    def deliver(e):
        for a in range(2):
            @pl.when(e == own)
            def _():
                to_self(a, e).start()

            @pl.when(e != own)
            def _():
                to_host(a, e).start()

    for a in range(2):
        ring(0, a, 1).start()
        ring(1, a, 1).start()
    deliver(plane)
    finish_rows = start_rows(plane, own, send_ref, rows_ref, tok_send, tok_recv)

    @pl.loop(1, 17)
    def _(step):
        for a in range(2):
            arrival(0, a, step).wait_recv()

            @pl.when(step < 16)
            def _():
                ring(0, a, step + 1).start()

            @pl.when(step < 16)
            def _():
                arrival(1, a, step).wait_recv()

            @pl.when(step < 15)
            def _():
                ring(1, a, step + 1).start()

        @pl.when(step % 4 == 0)
        def _():
            @pl.loop(0, 8)
            def _(i):
                j = (i + own) % 8
                away = step - 3 + j // 2

                @pl.when(j % 2 == 0)
                def _():
                    deliver((plane - away + 2 * PLANES) % PLANES)

                @pl.when((j % 2 == 1) & (away < 16))
                def _():
                    deliver((plane + away) % PLANES)

    finish_rows()

    @pl.loop(1, 17)
    def _(step):
        for a in range(2):
            ring(0, a, step).wait_send()

            @pl.when(step < 16)
            def _():
                ring(1, a, step).wait_send()

    @pl.loop(0, E)
    def _(e):
        there = pl.ds(
            pl.multiple_of((e % 16) // 8 * (FF // 2) + ((e % 8) // 4 * 8 + e % 4 * 2 + e // 16) * SLAB, SLAB),
            SLAB,
        )
        for a in range(2):
            @pl.when(e != own)
            def _():
                to_host(a, e).wait_send()

            pltpu.make_async_copy(held.at[a, e], full[a].at[there], host_recv.at[a, e]).wait()


def expert_kernel(factor, rows_ref, fin_ref, fout_ref, back_ref, grad_ref, x, d, out, inp):
    x[...] = rows_ref[:, 0:CAP].reshape(ROWS, 8, 128).reshape(ROWS, D)
    d[...] = rows_ref[:, CAP : 2 * CAP].reshape(ROWS, 8, 128).reshape(ROWS, D)
    out[...] = jnp.zeros_like(out)
    inp[...] = jnp.zeros_like(inp)

    @pl.loop(0, FF // FCHUNK)
    def _(c):
        units = pl.ds(pl.multiple_of(c * FCHUNK, FCHUNK), FCHUNK)
        wi = fin_ref[units, :]
        wo = fout_ref[units, :]
        v = dot_t(x[...], wi)
        t = jnp.tanh(gelu_scale * (v + gelu_cubic * v * v * v))
        act = (0.5 * v * (1.0 + t)).astype(BF16)
        slope = 0.5 * (1.0 + t) + 0.5 * v * (1.0 - t * t) * gelu_scale * (
            1.0 + 3.0 * gelu_cubic * v * v
        )
        dhid = (dot_t(d[...], wo) * slope).astype(BF16)
        out[...] += jnp.dot(act, wo, preferred_element_type=F32)
        inp[...] += jnp.dot(dhid, wi, preferred_element_type=F32)
        cols = pl.ds(pl.multiple_of(c % 2 * FCHUNK, FCHUNK), FCHUNK)
        g_in = (dot_cols(x[...], dhid) * factor).astype(BF16)
        grad_ref[c // 2, :, 0, :, cols] = g_in.reshape(16, 64, FCHUNK)
        g_out = (dot_cols(d[...], act) * factor).astype(BF16)
        grad_ref[c // 2, :, 1, :, cols] = g_out.reshape(16, 64, FCHUNK)

    back_ref[:, 0:CAP] = out[...].astype(BF16).reshape(ROWS, 8, 128).reshape(E, CAP, 8, 128)
    back_ref[:, CAP : 2 * CAP] = inp[...].astype(BF16).reshape(ROWS, 8, 128).reshape(E, CAP, 8, 128)


def scatter_kernel(
    back_ref, grad_ref, rows_ref, gin_ref, gout_ref,
    parts, up_got, up_held, down_got, down_held,
    tok_send, tok_recv, part_send, part_recv, up_send, up_recv, down_send, down_recv,
):
    plane, x_hi, dp, own = position()
    up, down = up_of(plane, x_hi), down_of(plane, x_hi)
    enter(plane, x_hi, own)

    def part(k):
        to = (own + k) % E
        dev = plane_device(to, plane)
        return pltpu.make_async_remote_copy(
            src_ref=grad_ref.at[(to % 16) // 8, dev["dp"]],
            dst_ref=parts.at[own],
            send_sem=part_send.at[k],
            recv_sem=part_recv.at[own],
            device_id=dev,
            device_id_type=MESH,
        )

    def own_part():
        return pltpu.make_async_copy(grad_ref.at[x_hi, dp], parts.at[own], part_recv.at[own])

    at_up = (plane + 16 - own + PLANES) % PLANES
    my_step = jnp.where(at_up < 16, at_up, 31 - at_up)

    def send_parts(window):
        @pl.when(my_step // 4 == window)
        def _():
            own_part().start()

            @pl.loop(1, E)
            def _(k):
                part(k).start()

    def await_part(e):
        pltpu.make_async_copy(grad_ref.at[x_hi, dp], parts.at[e], part_recv.at[e]).wait()

    def up_copy(a, step, first=False):
        e = (plane + 16) % PLANES
        return pltpu.make_async_remote_copy(
            src_ref=parts.at[e, a] if first else up_held.at[step, a],
            dst_ref=up_got.at[step, a],
            send_sem=up_send.at[a, step],
            recv_sem=up_recv.at[a, step],
            device_id=up,
            device_id_type=MESH,
        )

    def down_copy(a, step, first=False):
        e = (plane - 15 + PLANES) % PLANES
        return pltpu.make_async_remote_copy(
            src_ref=parts.at[e, a] if first else down_held.at[step, a],
            dst_ref=down_got.at[step, a],
            send_sem=down_send.at[a, step],
            recv_sem=down_recv.at[a, step],
            device_id=down,
            device_id_type=MESH,
        )

    send_parts(0)
    send_parts(1)
    finish_rows = start_rows(plane, own, back_ref, rows_ref, tok_send, tok_recv)
    await_part((plane + 16) % PLANES)
    await_part((plane - 15 + PLANES) % PLANES)
    for a in range(2):
        up_copy(a, 0, True).start()
        down_copy(a, 0, True).start()

    @pl.loop(1, 16)
    def _(t):
        @pl.when(t == 4)
        def _():
            send_parts(2)

        @pl.when(t == 8)
        def _():
            send_parts(3)

        eu = (plane + 16 - t) % PLANES
        ed = (plane - 15 + t + PLANES) % PLANES
        await_part(eu)

        @pl.when(t < 15)
        def _():
            await_part(ed)

        for a in range(2):
            up_copy(a, t - 1).wait_recv()
            up_held[t, a] = (up_got[t - 1, a].astype(F32) + parts[eu, a].astype(F32)).astype(BF16)
            up_copy(a, t).start()

            @pl.when(t < 15)
            def _():
                down_copy(a, t - 1).wait_recv()
                down_held[t, a] = (
                    down_got[t - 1, a].astype(F32) + parts[ed, a].astype(F32)
                ).astype(BF16)
                down_copy(a, t).start()

    await_part(plane)
    for a, ref in enumerate((gin_ref, gout_ref)):
        up_copy(a, 15).wait_recv()
        down_copy(a, 14).wait_recv()
        ref[...] = (
            up_got[15, a].astype(F32) + down_got[14, a].astype(F32) + parts[plane, a].astype(F32)
        )
    finish_rows()

    @pl.loop(1, E)
    def _(k):
        part(k).wait_send()

    for a in range(2):
        up_copy(a, 0, True).wait_send()
        down_copy(a, 0, True).wait_send()

    @pl.loop(1, 16)
    def _(t):
        for a in range(2):
            up_copy(a, t).wait_send()

            @pl.when(t < 15)
            def _():
                down_copy(a, t).wait_send()


def combine_kernel(rows_ref, pos_ref, gate_ref, cot_ref, layer_ref, ggrad_ref, igrad_ref):
    out_rows = rows_ref[:, 0:CAP].reshape(ROWS, 8, 128).reshape(ROWS, D)
    in_rows = rows_ref[:, CAP : 2 * CAP].reshape(ROWS, 8, 128).reshape(ROWS, D)
    slot_row = lax.broadcasted_iota(jnp.int32, (ROWS, TOK), 0)
    picks = [slot_row == pos_ref[k : k + 1, :] for k in range(2)]
    cot = cot_ref[...].astype(F32)
    layer = jnp.zeros((TOK, D), F32)
    for k in range(2):
        got = dot_cols(picks[k].astype(F32).astype(BF16), out_rows)
        layer = layer + gate_ref[:, k : k + 1] * got
        ggrad_ref[:, k : k + 1] = jnp.sum(cot * got, axis=1, keepdims=True)
    layer_ref[...] = layer.astype(BF16)
    both = (picks[0] | picks[1]).astype(F32).astype(BF16)
    igrad_ref[...] = dot_cols(both, in_rows).astype(BF16)


def local(tokens, gate_values, expert_ids, cotangent, weight_in, weight_out):
    tok_all = TOK * lax.axis_size("dp") * lax.axis_size("seq")
    factor = (E / (2.0 * tok_all)) ** 0.5
    shape = jax.ShapeDtypeStruct
    dma = pltpu.SemaphoreType.DMA
    rows_shape = shape((E, 2 * CAP, 8, 128), BF16)
    big = pltpu.CompilerParams(vmem_limit_bytes=60 << 20)
    send, pos = pl.pallas_call(
        pick_kernel,
        out_shape=(rows_shape, shape((2, TOK), jnp.int32)),
        in_specs=[VMEM] * 4,
        out_specs=(VMEM, VMEM),
        compiler_params=big,
    )(expert_ids.T, gate_values.T, tokens, cotangent)
    rows, full_in, full_out = pl.pallas_call(
        gather_kernel,
        out_shape=(rows_shape, shape((FF, D), BF16), shape((FF, D), BF16)),
        in_specs=[VMEM] * 3,
        out_specs=(VMEM,) * 3,
        scratch_shapes=[
            pltpu.VMEM((2, E, SLAB, D), BF16),
            dma((2,)), dma((E,)), dma((E,)),
            dma((2, 2, 17)), dma((2, 2, 17)), dma((2, E)), dma((2, E)),
        ],
        compiler_params=pltpu.CompilerParams(
            collective_id=0, has_side_effects=True, vmem_limit_bytes=60 << 20
        ),
    )(send, weight_in, weight_out)
    back, grads = pl.pallas_call(
        functools.partial(expert_kernel, factor),
        out_shape=(rows_shape, shape((2, 16, 2, 64, FF // 2), BF16)),
        in_specs=[VMEM] * 3,
        out_specs=(VMEM, VMEM),
        scratch_shapes=[
            pltpu.VMEM((ROWS, D), BF16), pltpu.VMEM((ROWS, D), BF16),
            pltpu.VMEM((ROWS, D), F32), pltpu.VMEM((ROWS, D), F32),
        ],
        compiler_params=big,
    )(rows, full_in, full_out)
    piece = (2, 64, FF // 2)
    returned, grad_in, grad_out = pl.pallas_call(
        scatter_kernel,
        out_shape=(rows_shape, shape((64, FF // 2), F32), shape((64, FF // 2), F32)),
        in_specs=[VMEM] * 2,
        out_specs=(VMEM,) * 3,
        scratch_shapes=[
            pltpu.VMEM((E,) + piece, BF16),
            pltpu.VMEM((16,) + piece, BF16), pltpu.VMEM((16,) + piece, BF16),
            pltpu.VMEM((16,) + piece, BF16), pltpu.VMEM((16,) + piece, BF16),
            dma((E,)), dma((E,)), dma((E,)), dma((E,)),
            dma((2, 16)), dma((2, 16)), dma((2, 16)), dma((2, 16)),
        ],
        compiler_params=pltpu.CompilerParams(
            collective_id=1, has_side_effects=True, vmem_limit_bytes=60 << 20
        ),
    )(back, grads)
    layer_out, gate_grad, input_grad = pl.pallas_call(
        combine_kernel,
        out_shape=(shape((TOK, D), BF16), shape((TOK, 2), F32), shape((TOK, D), BF16)),
        in_specs=[VMEM] * 4,
        out_specs=(VMEM,) * 3,
        compiler_params=big,
    )(returned, pos, gate_values, cotangent)
    return layer_out, gate_grad, input_grad, grad_in, grad_out


def solution(mesh):
    tok = P(("dp", "seq"), None)
    return jax.shard_map(
        local,
        mesh=mesh,
        in_specs=(tok, tok, tok, tok, P("seq", None), P("seq", None)),
        out_specs=(tok, tok, tok, P("dp", "seq"), P("dp", "seq")),
        check_vma=False,
    )
```

time: 903 us -> 260 us (0.29)
  waiting for transfers between devices: 740 us -> 0 us
  Pallas kernels: 0 us -> 256 us
  local copies, waits for them, and re-layouts: 67.3 us -> 3.54 us
  starting transfers between devices: 49 us -> 0 us
  other arithmetic: 19 us -> 0 us
  between operations: 14.4 us -> 0.68 us
  matrix products: 12.6 us -> 0 us
    all_to_all x4 -> x0, waiting for transfers between devices: 661 us -> none  [the longest x1 189 us: local(): lax.all_to_all(send_d, 'seq', split_axis=0, concat_axis=0, tiled=True)]
    pallas_call x0 -> x5, Pallas kernels: none -> 256 us  [the longest x1 134 us: local(): pl.pallas_call(scatter_kernel, out_shape=(rows_shape, shape((64, FF // 2)...]
    unnamed x2 -> x0, waiting for transfers between devices: 78.6 us -> none
    all_to_all x4 -> x0, starting transfers between devices: 48.9 us -> none  [the longest x1 31.9 us: local(): lax.all_to_all(send_x, 'seq', split_axis=0, concat_axis=0, tiled=True)]
    gather x9 -> x0, local copies, waits for them, and re-layouts: 24.4 us -> none  [the longest x4 6.27 us: collect(): summed = summed + flat_rows[row_at].astype(jnp.float32)]
    another operation x7 -> x0, local copies, waits for them, and re-layouts: 15.8 us -> none  [the longest x2 6.65 us: from_rows(): return jnp.transpose(grouped, (1, 0, 2, 3)).reshape(send_shape)]
    dot_general x6 -> x0, matrix products: 12.6 us -> none  [the longest x1 3.04 us: local(): jnp.einsum('krd,kfd->krf', rows_d, wout_local, preferred_element_type=jnp...]
  transfers between devices with their start and end apart: 5 -> 0, of which waited for: 5 -> 0; matrix products, arithmetic and copies ran while one was open for 6% -> 0% of each run, Pallas kernels for 0% -> 0%
where the time goes in v1:
time: 260 us
  Pallas kernels  256 us (98%)
  local copies, waits for them, and re-layouts  3.54 us (1%)
    pallas_call x1, Pallas kernels, local(): pl.pallas_call(scatter_kernel, out_shape=(rows_shape, shape((64, FF // 2)...  134 us
    pallas_call x1, Pallas kernels, local(): pl.pallas_call(gather_kernel, out_shape=(rows_shape, shape((FF, D), BF16)...  103 us
    pallas_call x1, Pallas kernels, local(): pl.pallas_call(functools.partial(expert_kernel, factor), out_shape=(rows_...  12 us

profile of v1, /device:TPU:24, one launch (start us, length us, event | category | flops | bytes accessed | tf_op | source)
XLA Modules:
  0.0 260.0 jit_solution(7663007406238150710)
XLA Ops:
  0.6 3.5 %shard_map.101 = (bf16[32,18,8,128]{3,2,1,0:T(8,128)(2,1)}, s32[2,128]{1,0:T(2,128)}) custom-call(s32[2,128]{1,0:T(2,128)} %bitcast.3, f32[2,128]{1,0:T(2,128)} %bitcast.2, bf16[128,1024]{1,0:T(8,128)(2,1)} %tok_ref.1, bf16[128,1024]{1,0:T(8,128)(2,1)} %cot_ref.3), custom_call_target="tpu_custom_call" | custom-call | tf_op jit(solution)/shard_map/pallas_call | solution.py:443
  4.2 103.2 %shard_map.102 = (bf16[32,18,8,128]{3,2,1,0:T(8,128)(2,1)}, bf16[1024,1024]{1,0:T(8,128)(2,1)}, bf16[1024,1024]{1,0:T(8,128)(2,1)}) custom-call(bf16[32,18,8,128]{3,2,1,0:T(8,128)(2,1)} %get-tuple-element.18.send_ref, bf16[512,1024]{1,0:T(8,128)(2,1)} %win_ref.1, bf16[512,1024]{1,0:T(8,128)(2,1)} %wout_ref.1), custom_call_target="tpu_custom_call" | custom-call | tf_op jit(solution)/shard_map/pallas_call | solution.py:450
  107.4 12.0 %shard_map.103 = (bf16[32,18,8,128]{3,2,1,0:T(8,128)(2,1)}, bf16[2,16,2,64,512]{4,3,2,1,0:T(8,128)(2,1)}) custom-call(bf16[32,18,8,128]{3,2,1,0:T(8,128)(2,1)} %get-tuple-element.19.rows_ref, bf16[1024,1024]{1,0:T(8,128)(2,1)} %get-tuple-element.20.fin_ref, bf16[1024,1024]{1,0:T(8,128)(2,1)} %get-tuple-element.21.fout_ref), custom_call_target="tpu_custom_call" | custom-call | tf_op jit(solution)/shard_map/pallas_call | solution.py:464
  119.4 0.0 copy-start.2
  119.4 134.0 %shard_map.104 = (bf16[32,18,8,128]{3,2,1,0:T(8,128)(2,1)}, f32[64,512]{1,0:T(8,128)}, f32[64,512]{1,0:T(8,128)}) custom-call(bf16[32,18,8,128]{3,2,1,0:T(8,128)(2,1)} %get-tuple-element.22.back_ref, bf16[2,16,2,64,512]{4,3,2,1,0:T(8,128)(2,1)} %get-tuple-element.23.grad_ref), custom_call_target="tpu_custom_call" | custom-call | tf_op jit(solution)/shard_map/pallas_call | solution.py:476
  253.4 0.0 copy-start.1
  253.4 0.0 copy-start
  253.4 0.0 copy-done.2
  253.4 0.7 copy.11.gate_ref
  254.2 3.0 %shard_map.105 = (bf16[128,1024]{1,0:T(8,128)(2,1)}, f32[128,2]{1,0:T(8,128)}, bf16[128,1024]{1,0:T(8,128)(2,1)}) custom-call(bf16[32,18,8,128]{3,2,1,0:T(8,128)(2,1)} %get-tuple-element.24.rows_ref, s32[2,128]{1,0:T(2,128)} %get-tuple-element.25.pos_ref, f32[128,2]{1,0:T(8,128)} %copy.11.gate_ref, bf16[128,1024]{1,0:T(8,128)(2,1)} %cot_ref.3), custom_call_target="tpu_custom_call" | custom-call | tf_op jit(solution)/shard_map/pallas_call | solution.py:492
  257.2 1.5 copy.12
  258.7 0.0 copy-done.1
  258.7 0.7 copy.15
  259.3 0.0 copy-done
  259.3 0.7 copy.16
Async XLA Ops:
  119.4 134.1 %copy-start.2 = (f32[128,2]{0,1:T(2,128)S(1)}, f32[128,2]{0,1:T(2,128)}, u32[]{:S(2)}) copy-start(f32[128,2]{0,1:T(2,128)} %param.7) | copy-start | bytes 3076
  253.4 5.3 %copy-start.1 = (f32[64,512]{1,0:T(8,128)S(1)}, f32[64,512]{1,0:T(8,128)}, u32[]{:S(2)}) copy-start(f32[64,512]{1,0:T(8,128)} %get-tuple-element.44) | copy-start | bytes 393220
  253.4 5.9 %copy-start = (f32[64,512]{1,0:T(8,128)S(1)}, f32[64,512]{1,0:T(8,128)}, u32[]{:S(2)}) copy-start(f32[64,512]{1,0:T(8,128)} %get-tuple-element.45) | copy-start | bytes 393220

commit v2 on v1

v2 whole, which is shorter than its diff:
```python
import functools

import jax
import jax.numpy as jnp
from jax import lax
from jax.experimental import pallas as pl
from jax.experimental.pallas import tpu as pltpu
from jax.sharding import PartitionSpec as P

MESH = pl.DeviceIdType.MESH
BF16 = jnp.bfloat16
F32 = jnp.float32

D = 1024
E = 32
FF = 1024
CAP = 9
TOK = 128
ROWS = E * CAP
PLANES = 32
PAIR = 64
PIECES = 4
AHEAD = 8
LAG = 0
WIN = 1
FCHUNK = 256

gelu_scale = 0.7978845608028654
gelu_cubic = 0.044715

VMEM = pl.BlockSpec(memory_space=pltpu.VMEM)


def plane_device(expert, plane):
    x = expert % 4
    y = (expert // 4 + x) % 4
    return {"dp": x % 2 * 8 + y * 2 + expert // 16 % 2, "seq": plane * 2 + x // 2}


def position():
    seq = lax.axis_index("seq")
    dp = lax.axis_index("dp")
    plane = seq // 2
    x_hi = seq % 2
    x = x_hi * 2 + dp // 8
    own = x + (dp // 2 % 4 - x + 4) % 4 * 4 + 16 * (dp % 2)
    return plane, x_hi, dp, own


def up_of(plane, x_hi):
    return {"seq": (plane + 1) % PLANES * 2 + x_hi}


def down_of(plane, x_hi):
    return {"seq": (plane + PLANES - 1) % PLANES * 2 + x_hi}


def enter(plane, x_hi, own):
    barrier = pltpu.get_barrier_semaphore()
    pl.semaphore_signal(barrier, inc=1, device_id=up_of(plane, x_hi), device_id_type=MESH)
    pl.semaphore_signal(barrier, inc=1, device_id=down_of(plane, x_hi), device_id_type=MESH)

    @pl.loop(1, E)
    def _(k):
        pl.semaphore_signal(
            barrier, inc=1, device_id=plane_device((own + k) % E, plane), device_id_type=MESH
        )

    pl.semaphore_wait(barrier, E + 1)


def dot_t(a, b):
    return lax.dot_general(a, b, (((1,), (1,)), ((), ())), preferred_element_type=F32)


def dot_cols(a, b):
    return lax.dot_general(a, b, (((0,), (0,)), ((), ())), preferred_element_type=F32)


def pick_kernel(ids_ref, gate_ref, tok_ref, cot_ref, send_ref, pos_ref):
    expert = lax.broadcasted_iota(jnp.int32, (E, TOK), 0)
    hot = [(expert == ids_ref[k : k + 1, :]).astype(F32) for k in range(2)]
    row = lax.broadcasted_iota(jnp.int32, (TOK, TOK), 0)
    col = lax.broadcasted_iota(jnp.int32, (TOK, TOK), 1)
    earlier = (row < col).astype(BF16)
    before = jnp.dot((hot[0] + hot[1]).astype(BF16), earlier, preferred_element_type=F32)
    slot_row = lax.broadcasted_iota(jnp.int32, (ROWS, TOK), 0)
    picks = []
    gates = jnp.zeros((ROWS, 1), F32)
    for k in range(2):
        slot = jnp.sum(before * hot[k], axis=0, keepdims=True).astype(jnp.int32)
        at = ids_ref[k : k + 1, :] * CAP + slot
        pos_ref[k : k + 1, :] = at
        pick = slot_row == at
        picks.append(pick)
        gates = gates + jnp.sum(
            jnp.where(pick, gate_ref[k : k + 1, :], 0.0), axis=1, keepdims=True
        )
    both = (picks[0] | picks[1]).astype(F32).astype(BF16)
    x_rows = jnp.dot(both, tok_ref[...], preferred_element_type=F32).astype(BF16)
    send_ref[:, 0:CAP] = x_rows.reshape(ROWS, 8, 128).reshape(E, CAP, 8, 128)
    d_rows = (jnp.dot(both, cot_ref[...], preferred_element_type=F32) * gates).astype(BF16)
    send_ref[:, CAP : 2 * CAP] = d_rows.reshape(ROWS, 8, 128).reshape(E, CAP, 8, 128)


def start_rows(plane, own, src, dst, ssem, rsem):
    keep = pltpu.make_async_copy(src.at[own], dst.at[own], ssem.at[0])
    keep.start()

    def copy(k):
        to = (own + k) % E
        return pltpu.make_async_remote_copy(
            src_ref=src.at[to],
            dst_ref=dst.at[own],
            send_sem=ssem.at[k],
            recv_sem=rsem.at[k],
            device_id=plane_device(to, plane),
            device_id_type=MESH,
        )

    @pl.loop(1, E)
    def _(k):
        copy(k).start()

    def finish():
        keep.wait()

        @pl.loop(1, E)
        def _(k):
            copy(k).wait()

    return finish


def gather_kernel(
    send_ref, win_ref, wout_ref, rows_ref, fin_ref, fout_ref,
    held, own_sem, tok_send, tok_recv, ring_send, ring_recv, host_send, host_recv,
):
    plane, x_hi, dp, own = position()
    core = dp % 2
    chip = x_hi * 8 + dp // 2
    steps = 16 - core
    toward = 1 - 2 * core
    onward = {"seq": (plane + toward + PLANES) % PLANES * 2 + x_hi}
    slab = pl.ds(pl.multiple_of(dp // 2 * PAIR, PAIR), PAIR)
    place = pl.ds(pl.multiple_of(chip * PAIR, PAIR), PAIR)
    full = (fin_ref, fout_ref)
    mine = [
        pltpu.make_async_copy(ref.at[slab], held.at[a, 0], own_sem.at[a])
        for a, ref in enumerate((win_ref, wout_ref))
    ]
    for c in mine:
        c.start()
    enter(plane, x_hi, own)
    for c in mine:
        c.wait()
    cut = PAIR // PIECES

    def ring(a, h, step):
        return pltpu.make_async_remote_copy(
            src_ref=held.at[a, step - 1, pl.ds(h * cut, cut)],
            dst_ref=held.at[a, step, pl.ds(h * cut, cut)],
            send_sem=ring_send.at[a, h, step],
            recv_sem=ring_recv.at[a, h, step],
            device_id=onward,
            device_id_type=MESH,
        )

    def to_host(a, step):
        return pltpu.make_async_remote_copy(
            src_ref=held.at[a, step],
            dst_ref=full[a].at[place],
            send_sem=host_send.at[a, step],
            recv_sem=host_recv.at[a, chip],
            device_id=plane_device((plane - toward * step + 2 * PLANES) % PLANES, plane),
            device_id_type=MESH,
        )

    def is_own(step):
        return (plane - toward * step + 2 * PLANES) % PLANES == own

    def deliver(step):
        for a in range(2):
            @pl.when(is_own(step))
            def _():
                pltpu.make_async_copy(
                    held.at[a, step], full[a].at[place], host_recv.at[a, chip]
                ).start()

            @pl.when(~is_own(step))
            def _():
                to_host(a, step).start()

    for h in range(PIECES):
        for a in range(2):
            ring(a, h, 1).start()

    @pl.when(core == 1)
    def _():
        deliver(0)

    finish_rows = start_rows(plane, own, send_ref, rows_ref, tok_send, tok_recv)

    @pl.loop(1, 17)
    def _(step):
        @pl.when(step <= steps)
        def _():
            for h in range(PIECES):
                for a in range(2):
                    ring(a, h, step).wait_recv()

                    @pl.when(step < steps)
                    def _():
                        ring(a, h, step + 1).start()

        @pl.when(step % WIN == 0)
        def _():
            @pl.loop(0, WIN)
            def _(i):
                at = step - WIN + 1 + (i + own) % WIN

                @pl.when(at <= steps)
                def _():
                    deliver(at)

    finish_rows()

    @pl.loop(1, 17)
    def _(step):
        @pl.when(step <= steps)
        def _():
            for a in range(2):
                for h in range(PIECES):
                    ring(a, h, step).wait_send()

    @pl.loop(0, 17)
    def _(step):
        for a in range(2):
            @pl.when((step <= steps) & ((step > 0) | (core == 1)) & ~is_own(step))
            def _():
                to_host(a, step).wait_send()

    @pl.loop(0, 16)
    def _(c):
        there = pl.ds(pl.multiple_of(c * PAIR, PAIR), PAIR)
        for a in range(2):
            pltpu.make_async_copy(held.at[a, 0], full[a].at[there], host_recv.at[a, c]).wait()


def expert_kernel(factor, rows_ref, fin_ref, fout_ref, back_ref, grad_ref, x, d, out, inp):
    x[...] = rows_ref[:, 0:CAP].reshape(ROWS, 8, 128).reshape(ROWS, D)
    d[...] = rows_ref[:, CAP : 2 * CAP].reshape(ROWS, 8, 128).reshape(ROWS, D)
    out[...] = jnp.zeros_like(out)
    inp[...] = jnp.zeros_like(inp)

    @pl.loop(0, FF // FCHUNK)
    def _(c):
        units = pl.ds(pl.multiple_of(c * FCHUNK, FCHUNK), FCHUNK)
        wi = fin_ref[units, :]
        wo = fout_ref[units, :]
        v = dot_t(x[...], wi)
        t = jnp.tanh(gelu_scale * (v + gelu_cubic * v * v * v))
        act = (0.5 * v * (1.0 + t)).astype(BF16)
        slope = 0.5 * (1.0 + t) + 0.5 * v * (1.0 - t * t) * gelu_scale * (
            1.0 + 3.0 * gelu_cubic * v * v
        )
        dhid = (dot_t(d[...], wo) * slope).astype(BF16)
        out[...] += jnp.dot(act, wo, preferred_element_type=F32)
        inp[...] += jnp.dot(dhid, wi, preferred_element_type=F32)
        cols = pl.ds(pl.multiple_of(c % 2 * FCHUNK, FCHUNK), FCHUNK)
        g_in = (dot_cols(x[...], dhid) * factor).astype(BF16)
        grad_ref[c // 2, :, :, 0, :, cols] = g_in.reshape(8, PIECES, 128 // PIECES, FCHUNK)
        g_out = (dot_cols(d[...], act) * factor).astype(BF16)
        grad_ref[c // 2, :, :, 1, :, cols] = g_out.reshape(8, PIECES, 128 // PIECES, FCHUNK)

    back_ref[:, 0:CAP] = out[...].astype(BF16).reshape(ROWS, 8, 128).reshape(E, CAP, 8, 128)
    back_ref[:, CAP : 2 * CAP] = inp[...].astype(BF16).reshape(ROWS, 8, 128).reshape(E, CAP, 8, 128)


def scatter_kernel(
    back_ref, grad_ref, rows_ref, gin_ref, gout_ref,
    parts, got, held, other,
    tok_send, tok_recv, part_send, part_recv, ring_send, ring_recv, swap_send, swap_recv,
):
    plane, x_hi, dp, own = position()
    core = dp % 2
    chip = x_hi * 8 + dp // 2
    steps = 16 - core
    toward = 1 - 2 * core
    onward = {"seq": (plane + toward + PLANES) % PLANES * 2 + x_hi}
    cut = 2 * 64 // PIECES
    enter(plane, x_hi, own)

    at_up = (plane + 16 - own + PLANES) % PLANES
    goes_down = at_up // 17
    my_step = at_up + goes_down * (31 - 2 * at_up)

    def part(k, h):
        to = (chip + k) % 16
        return pltpu.make_async_remote_copy(
            src_ref=grad_ref.at[to // 8, to % 8, h],
            dst_ref=parts.at[my_step, h],
            send_sem=part_send.at[h, k],
            recv_sem=part_recv.at[h, my_step],
            device_id={"dp": to % 8 * 2 + goes_down, "seq": plane * 2 + to // 8},
            device_id_type=MESH,
        )

    def send_parts():
        @pl.loop(0, PIECES)
        def _(h):
            @pl.when(goes_down == core)
            def _():
                pltpu.make_async_copy(
                    grad_ref.at[x_hi, dp // 2, h], parts.at[my_step, h], part_recv.at[h, my_step]
                ).start()

            @pl.when(goes_down != core)
            def _():
                part(0, h).start()

            @pl.loop(1, 16)
            def _(k):
                part(k, h).start()

    def await_part(step, h):
        pltpu.make_async_copy(
            grad_ref.at[x_hi, dp // 2, h], parts.at[step, h], part_recv.at[h, step]
        ).wait()

    def ring(h, step, first=False):
        return pltpu.make_async_remote_copy(
            src_ref=parts.at[0, h] if first else held.at[step, h],
            dst_ref=got.at[step, h],
            send_sem=ring_send.at[h, step],
            recv_sem=ring_recv.at[h, step],
            device_id=onward,
            device_id_type=MESH,
        )

    @pl.when(my_step < AHEAD)
    def _():
        send_parts()

    finish_rows = start_rows(plane, own, back_ref, rows_ref, tok_send, tok_recv)

    @pl.loop(0, 16 + LAG * (PIECES - 1))
    def _(tick):
        @pl.when(my_step == tick + AHEAD)
        def _():
            send_parts()

        for h in range(PIECES):
            t = tick - LAG * h

            @pl.when(t == 0)
            def _():
                await_part(0, h)
                ring(h, 0, True).start()

            @pl.when((t > 0) & (t < steps))
            def _():
                await_part(t, h)
                ring(h, t - 1).wait_recv()
                held[t, h] = (got[t - 1, h].astype(F32) + parts[t, h].astype(F32)).astype(BF16)
                ring(h, t).start()

    @pl.when(my_step >= 16 + LAG * (PIECES - 1) + AHEAD)
    def _():
        send_parts()

    for h in range(PIECES):
        ring(h, steps - 1).wait_recv()

        @pl.when(core == 0)
        def _():
            await_part(16, h)
            held[0, h] = (got[15, h].astype(F32) + parts[16, h].astype(F32)).astype(BF16)

        @pl.when(core == 1)
        def _():
            held[0, h] = got[14, h]

    half = PIECES // 2
    mine = pl.ds(core * half, half)
    theirs = pl.ds(half - core * half, half)
    swap = pltpu.make_async_remote_copy(
        src_ref=held.at[0, theirs],
        dst_ref=other,
        send_sem=swap_send,
        recv_sem=swap_recv,
        device_id={"dp": dp + 1 - 2 * core},
        device_id_type=MESH,
    )
    swap.start()
    swap.wait()
    total = held[0, mine].astype(F32) + other[...].astype(F32)
    for a, ref in enumerate((gin_ref, gout_ref)):
        ref[...] = total[:, a].reshape(64, FF // 2)
    finish_rows()

    @pl.loop(0, PIECES)
    def _(h):
        @pl.when(goes_down != core)
        def _():
            part(0, h).wait_send()

        @pl.loop(1, 16)
        def _(k):
            part(k, h).wait_send()

    for h in range(PIECES):
        ring(h, 0, True).wait_send()

    @pl.loop(1, 16)
    def _(t):
        @pl.when(t < steps)
        def _():
            for h in range(PIECES):
                ring(h, t).wait_send()


def combine_kernel(rows_ref, pos_ref, gate_ref, cot_ref, layer_ref, ggrad_ref, igrad_ref):
    out_rows = rows_ref[:, 0:CAP].reshape(ROWS, 8, 128).reshape(ROWS, D)
    in_rows = rows_ref[:, CAP : 2 * CAP].reshape(ROWS, 8, 128).reshape(ROWS, D)
    slot_row = lax.broadcasted_iota(jnp.int32, (ROWS, TOK), 0)
    picks = [slot_row == pos_ref[k : k + 1, :] for k in range(2)]
    cot = cot_ref[...].astype(F32)
    layer = jnp.zeros((TOK, D), F32)
    for k in range(2):
        got = dot_cols(picks[k].astype(F32).astype(BF16), out_rows)
        layer = layer + gate_ref[:, k : k + 1] * got
        ggrad_ref[:, k : k + 1] = jnp.sum(cot * got, axis=1, keepdims=True)
    layer_ref[...] = layer.astype(BF16)
    both = (picks[0] | picks[1]).astype(F32).astype(BF16)
    igrad_ref[...] = dot_cols(both, in_rows).astype(BF16)


def local(tokens, gate_values, expert_ids, cotangent, weight_in, weight_out):
    tok_all = TOK * lax.axis_size("dp") * lax.axis_size("seq")
    factor = (E / (2.0 * tok_all)) ** 0.5
    shape = jax.ShapeDtypeStruct
    piece = (PIECES, 2, 128 // PIECES, FF // 2)
    dma = pltpu.SemaphoreType.DMA
    rows_shape = shape((E, 2 * CAP, 8, 128), BF16)
    big = pltpu.CompilerParams(vmem_limit_bytes=60 << 20)
    send, pos = pl.pallas_call(
        pick_kernel,
        out_shape=(rows_shape, shape((2, TOK), jnp.int32)),
        in_specs=[VMEM] * 4,
        out_specs=(VMEM, VMEM),
        compiler_params=big,
    )(expert_ids.T, gate_values.T, tokens, cotangent)
    rows, full_in, full_out = pl.pallas_call(
        gather_kernel,
        out_shape=(rows_shape, shape((FF, D), BF16), shape((FF, D), BF16)),
        in_specs=[VMEM] * 3,
        out_specs=(VMEM,) * 3,
        scratch_shapes=[
            pltpu.VMEM((2, 17, PAIR, D), BF16),
            dma((2,)), dma((E,)), dma((E,)),
            dma((2, PIECES, 17)), dma((2, PIECES, 17)), dma((2, 17)), dma((2, 16)),
        ],
        compiler_params=pltpu.CompilerParams(
            collective_id=0, has_side_effects=True, vmem_limit_bytes=60 << 20
        ),
    )(send, weight_in, weight_out)
    back, grads = pl.pallas_call(
        functools.partial(expert_kernel, factor),
        out_shape=(rows_shape, shape((2, 8) + piece, BF16)),
        in_specs=[VMEM] * 3,
        out_specs=(VMEM, VMEM),
        scratch_shapes=[
            pltpu.VMEM((ROWS, D), BF16), pltpu.VMEM((ROWS, D), BF16),
            pltpu.VMEM((ROWS, D), F32), pltpu.VMEM((ROWS, D), F32),
        ],
        compiler_params=big,
    )(rows, full_in, full_out)
    returned, grad_in, grad_out = pl.pallas_call(
        scatter_kernel,
        out_shape=(rows_shape, shape((64, FF // 2), F32), shape((64, FF // 2), F32)),
        in_specs=[VMEM] * 2,
        out_specs=(VMEM,) * 3,
        scratch_shapes=[
            pltpu.VMEM((17,) + piece, BF16),
            pltpu.VMEM((16,) + piece, BF16), pltpu.VMEM((16,) + piece, BF16),
            pltpu.VMEM((PIECES // 2,) + piece[1:], BF16),
            dma((E,)), dma((E,)), dma((PIECES, 16)), dma((PIECES, 17)),
            dma((PIECES, 16)), dma((PIECES, 16)), dma(()), dma(()),
        ],
        compiler_params=pltpu.CompilerParams(
            collective_id=1, has_side_effects=True, vmem_limit_bytes=60 << 20
        ),
    )(back, grads)
    layer_out, gate_grad, input_grad = pl.pallas_call(
        combine_kernel,
        out_shape=(shape((TOK, D), BF16), shape((TOK, 2), F32), shape((TOK, D), BF16)),
        in_specs=[VMEM] * 4,
        out_specs=(VMEM,) * 3,
        compiler_params=big,
    )(returned, pos, gate_values, cotangent)
    return layer_out, gate_grad, input_grad, grad_in, grad_out


def solution(mesh):
    tok = P(("dp", "seq"), None)
    return jax.shard_map(
        local,
        mesh=mesh,
        in_specs=(tok, tok, tok, tok, P("seq", None), P("seq", None)),
        out_specs=(tok, tok, tok, P("dp", "seq"), P("dp", "seq")),
        check_vma=False,
    )
```

time: 260 us -> 241 us (0.927); the launches traced: 260 us -> 237 us
  Pallas kernels: 256 us -> 233 us
    pallas_call x1, Pallas kernels: 134 us -> 114 us  [local(): pl.pallas_call(scatter_kernel, out_shape=(rows_shape, shape((64, FF // 2)...]
where the time goes in v2:
time: 241 us; the launch traced here: 237 us
  Pallas kernels  233 us (97%)
  local copies, waits for them, and re-layouts  3.54 us (1%)
    pallas_call x1, Pallas kernels, local(): pl.pallas_call(scatter_kernel, out_shape=(rows_shape, shape((64, FF // 2)...  114 us
    pallas_call x1, Pallas kernels, local(): pl.pallas_call(gather_kernel, out_shape=(rows_shape, shape((FF, D), BF16)...  101 us
    pallas_call x1, Pallas kernels, local(): pl.pallas_call(functools.partial(expert_kernel, factor), out_shape=(rows_...  11.9 us

profile of v2, /device:TPU:24, one launch (start us, length us, event | category | flops | bytes accessed | tf_op | source)
XLA Modules:
  0.0 237.3 jit_solution(2505241400866391197)
XLA Ops:
  0.6 3.5 %shard_map.101 = (bf16[32,18,8,128]{3,2,1,0:T(8,128)(2,1)}, s32[2,128]{1,0:T(2,128)}) custom-call(s32[2,128]{1,0:T(2,128)} %bitcast.3, f32[2,128]{1,0:T(2,128)} %bitcast.2, bf16[128,1024]{1,0:T(8,128)(2,1)} %tok_ref.1, bf16[128,1024]{1,0:T(8,128)(2,1)} %cot_ref.3), custom_call_target="tpu_custom_call" | custom-call | tf_op jit(solution)/shard_map/pallas_call | solution.py:447
  4.2 100.8 %shard_map.102 = (bf16[32,18,8,128]{3,2,1,0:T(8,128)(2,1)}, bf16[1024,1024]{1,0:T(8,128)(2,1)}, bf16[1024,1024]{1,0:T(8,128)(2,1)}) custom-call(bf16[32,18,8,128]{3,2,1,0:T(8,128)(2,1)} %get-tuple-element.18.send_ref, bf16[512,1024]{1,0:T(8,128)(2,1)} %win_ref.1, bf16[512,1024]{1,0:T(8,128)(2,1)} %wout_ref.1), custom_call_target="tpu_custom_call" | custom-call | tf_op jit(solution)/shard_map/pallas_call | solution.py:454
  104.9 11.9 %shard_map.103 = (bf16[32,18,8,128]{3,2,1,0:T(8,128)(2,1)}, bf16[2,8,4,2,32,512]{5,4,3,2,1,0:T(8,128)(2,1)}) custom-call(bf16[32,18,8,128]{3,2,1,0:T(8,128)(2,1)} %get-tuple-element.19.rows_ref, bf16[1024,1024]{1,0:T(8,128)(2,1)} %get-tuple-element.20.fin_ref, bf16[1024,1024]{1,0:T(8,128)(2,1)} %get-tuple-element.21.fout_ref), custom_call_target="tpu_custom_call" | custom-call | tf_op jit(solution)/shard_map/pallas_call | solution.py:468
  116.9 0.0 copy-start.2
  116.9 113.9 %shard_map.104 = (bf16[32,18,8,128]{3,2,1,0:T(8,128)(2,1)}, f32[64,512]{1,0:T(8,128)}, f32[64,512]{1,0:T(8,128)}) custom-call(bf16[32,18,8,128]{3,2,1,0:T(8,128)(2,1)} %get-tuple-element.22.back_ref, bf16[2,8,4,2,32,512]{5,4,3,2,1,0:T(8,128)(2,1)} %get-tuple-element.23.grad_ref), custom_call_target="tpu_custom_call" | custom-call | tf_op jit(solution)/shard_map/pallas_call | solution.py:479
  230.8 0.0 copy-start.1
  230.8 0.0 copy-start
  230.8 0.0 copy-done.2
  230.8 0.7 copy.11.gate_ref
  231.5 3.0 %shard_map.105 = (bf16[128,1024]{1,0:T(8,128)(2,1)}, f32[128,2]{1,0:T(8,128)}, bf16[128,1024]{1,0:T(8,128)(2,1)}) custom-call(bf16[32,18,8,128]{3,2,1,0:T(8,128)(2,1)} %get-tuple-element.24.rows_ref, s32[2,128]{1,0:T(2,128)} %get-tuple-element.25.pos_ref, f32[128,2]{1,0:T(8,128)} %copy.11.gate_ref, bf16[128,1024]{1,0:T(8,128)(2,1)} %cot_ref.3), custom_call_target="tpu_custom_call" | custom-call | tf_op jit(solution)/shard_map/pallas_call | solution.py:495
  234.5 1.5 copy.12
  236.0 0.0 copy-done.1
  236.0 0.7 copy.15
  236.7 0.0 copy-done
  236.7 0.7 copy.16
Async XLA Ops:
  116.9 113.9 %copy-start.2 = (f32[128,2]{0,1:T(2,128)S(1)}, f32[128,2]{0,1:T(2,128)}, u32[]{:S(2)}) copy-start(f32[128,2]{0,1:T(2,128)} %param.7) | copy-start | bytes 3076
  230.8 5.2 %copy-start.1 = (f32[64,512]{1,0:T(8,128)S(1)}, f32[64,512]{1,0:T(8,128)}, u32[]{:S(2)}) copy-start(f32[64,512]{1,0:T(8,128)} %get-tuple-element.44) | copy-start | bytes 393220
  230.8 5.9 %copy-start = (f32[64,512]{1,0:T(8,128)S(1)}, f32[64,512]{1,0:T(8,128)}, u32[]{:S(2)}) copy-start(f32[64,512]{1,0:T(8,128)} %get-tuple-element.45) | copy-start | bytes 393220

commit v3 on v2

--- a/solution.py
+++ b/solution.py
@@ -66,7 +66,10 @@
             barrier, inc=1, device_id=plane_device((own + k) % E, plane), device_id_type=MESH
         )
 
-    pl.semaphore_wait(barrier, E + 1)
+    def ready():
+        pl.semaphore_wait(barrier, E + 1)
+
+    return ready
 
 
 def dot_t(a, b):
@@ -77,7 +80,7 @@
     return lax.dot_general(a, b, (((0,), (0,)), ((), ())), preferred_element_type=F32)
 
 
-def pick_kernel(ids_ref, gate_ref, tok_ref, cot_ref, send_ref, pos_ref):
+def pick_rows(ids_ref, gate_ref, tok_ref, cot_ref, send_ref, pos_ref):
     expert = lax.broadcasted_iota(jnp.int32, (E, TOK), 0)
     hot = [(expert == ids_ref[k : k + 1, :]).astype(F32) for k in range(2)]
     row = lax.broadcasted_iota(jnp.int32, (TOK, TOK), 0)
@@ -133,8 +136,8 @@
 
 
 def gather_kernel(
-    send_ref, win_ref, wout_ref, rows_ref, fin_ref, fout_ref,
-    held, own_sem, tok_send, tok_recv, ring_send, ring_recv, host_send, host_recv,
+    ids_ref, gate_ref, tok_ref, cot_ref, win_ref, wout_ref, rows_ref, fin_ref, fout_ref, pos_ref,
+    send_ref, held, own_sem, tok_send, tok_recv, ring_send, ring_recv, host_send, host_recv,
 ):
     plane, x_hi, dp, own = position()
     core = dp % 2
@@ -151,9 +154,11 @@
     ]
     for c in mine:
         c.start()
-    enter(plane, x_hi, own)
+    ready = enter(plane, x_hi, own)
+    pick_rows(ids_ref, gate_ref, tok_ref, cot_ref, send_ref, pos_ref)
     for c in mine:
         c.wait()
+    ready()
     cut = PAIR // PIECES
 
     def ring(a, h, step):
@@ -247,9 +252,11 @@
             pltpu.make_async_copy(held.at[a, 0], full[a].at[there], host_recv.at[a, c]).wait()
 
 
-def expert_kernel(factor, rows_ref, fin_ref, fout_ref, back_ref, grad_ref, x, d, out, inp):
+def work_expert(factor, rows_ref, fin_ref, fout_ref, back_ref, grad_ref, x, d, xt, dt, out, inp):
     x[...] = rows_ref[:, 0:CAP].reshape(ROWS, 8, 128).reshape(ROWS, D)
     d[...] = rows_ref[:, CAP : 2 * CAP].reshape(ROWS, 8, 128).reshape(ROWS, D)
+    xt[...] = x[...].T
+    dt[...] = d[...].T
     out[...] = jnp.zeros_like(out)
     inp[...] = jnp.zeros_like(inp)
 
@@ -268,9 +275,9 @@
         out[...] += jnp.dot(act, wo, preferred_element_type=F32)
         inp[...] += jnp.dot(dhid, wi, preferred_element_type=F32)
         cols = pl.ds(pl.multiple_of(c % 2 * FCHUNK, FCHUNK), FCHUNK)
-        g_in = (dot_cols(x[...], dhid) * factor).astype(BF16)
+        g_in = (jnp.dot(xt[...], dhid, preferred_element_type=F32) * factor).astype(BF16)
         grad_ref[c // 2, :, :, 0, :, cols] = g_in.reshape(8, PIECES, 128 // PIECES, FCHUNK)
-        g_out = (dot_cols(d[...], act) * factor).astype(BF16)
+        g_out = (jnp.dot(dt[...], act, preferred_element_type=F32) * factor).astype(BF16)
         grad_ref[c // 2, :, :, 1, :, cols] = g_out.reshape(8, PIECES, 128 // PIECES, FCHUNK)
 
     back_ref[:, 0:CAP] = out[...].astype(BF16).reshape(ROWS, 8, 128).reshape(E, CAP, 8, 128)
@@ -278,8 +285,8 @@
 
 
 def scatter_kernel(
-    back_ref, grad_ref, rows_ref, gin_ref, gout_ref,
-    parts, got, held, other,
+    factor, in_ref, fin_ref, fout_ref, rows_ref, sum_ref,
+    back_ref, grad_ref, x, d, xt, dt, out, inp, parts, got, held, other,
     tok_send, tok_recv, part_send, part_recv, ring_send, ring_recv, swap_send, swap_recv,
 ):
     plane, x_hi, dp, own = position()
@@ -289,7 +296,9 @@
     toward = 1 - 2 * core
     onward = {"seq": (plane + toward + PLANES) % PLANES * 2 + x_hi}
     cut = 2 * 64 // PIECES
-    enter(plane, x_hi, own)
+    ready = enter(plane, x_hi, own)
+    work_expert(factor, in_ref, fin_ref, fout_ref, back_ref, grad_ref, x, d, xt, dt, out, inp)
+    ready()
 
     at_up = (plane + 16 - own + PLANES) % PLANES
     goes_down = at_up // 17
@@ -394,9 +403,7 @@
     )
     swap.start()
     swap.wait()
-    total = held[0, mine].astype(F32) + other[...].astype(F32)
-    for a, ref in enumerate((gin_ref, gout_ref)):
-        ref[...] = total[:, a].reshape(64, FF // 2)
+    sum_ref[...] = held[0, mine].astype(F32) + other[...].astype(F32)
     finish_rows()
 
     @pl.loop(0, PIECES)
@@ -420,17 +427,24 @@
                 ring(h, t).wait_send()
 
 
-def combine_kernel(rows_ref, pos_ref, gate_ref, cot_ref, layer_ref, ggrad_ref, igrad_ref):
+def combine_kernel(
+    rows_ref, sum_ref, pos_ref, gate_ref, cot_ref, layer_ref, ggrad_ref, igrad_ref, gin_ref, gout_ref
+):
+    for a, ref in enumerate((gin_ref, gout_ref)):
+        ref[...] = sum_ref[:, a].reshape(64, FF // 2)
     out_rows = rows_ref[:, 0:CAP].reshape(ROWS, 8, 128).reshape(ROWS, D)
     in_rows = rows_ref[:, CAP : 2 * CAP].reshape(ROWS, 8, 128).reshape(ROWS, D)
     slot_row = lax.broadcasted_iota(jnp.int32, (ROWS, TOK), 0)
     picks = [slot_row == pos_ref[k : k + 1, :] for k in range(2)]
     cot = cot_ref[...].astype(F32)
     layer = jnp.zeros((TOK, D), F32)
+    gates = gate_ref[...].T
+    dots = []
     for k in range(2):
         got = dot_cols(picks[k].astype(F32).astype(BF16), out_rows)
-        layer = layer + gate_ref[:, k : k + 1] * got
-        ggrad_ref[:, k : k + 1] = jnp.sum(cot * got, axis=1, keepdims=True)
+        layer = layer + gates[:, k : k + 1] * got
+        dots.append(jnp.sum(cot * got, axis=1, keepdims=True))
+    ggrad_ref[...] = jnp.concatenate(dots, axis=1).T
     layer_ref[...] = layer.astype(BF16)
     both = (picks[0] | picks[1]).astype(F32).astype(BF16)
     igrad_ref[...] = dot_cols(both, in_rows).astype(BF16)
@@ -444,19 +458,15 @@
     dma = pltpu.SemaphoreType.DMA
     rows_shape = shape((E, 2 * CAP, 8, 128), BF16)
     big = pltpu.CompilerParams(vmem_limit_bytes=60 << 20)
-    send, pos = pl.pallas_call(
-        pick_kernel,
-        out_shape=(rows_shape, shape((2, TOK), jnp.int32)),
-        in_specs=[VMEM] * 4,
-        out_specs=(VMEM, VMEM),
-        compiler_params=big,
-    )(expert_ids.T, gate_values.T, tokens, cotangent)
-    rows, full_in, full_out = pl.pallas_call(
+    rows, full_in, full_out, pos = pl.pallas_call(
         gather_kernel,
-        out_shape=(rows_shape, shape((FF, D), BF16), shape((FF, D), BF16)),
-        in_specs=[VMEM] * 3,
-        out_specs=(VMEM,) * 3,
+        out_shape=(
+            rows_shape, shape((FF, D), BF16), shape((FF, D), BF16), shape((2, TOK), jnp.int32)
+        ),
+        in_specs=[VMEM] * 6,
+        out_specs=(VMEM,) * 4,
         scratch_shapes=[
+            pltpu.VMEM(rows_shape.shape, BF16),
             pltpu.VMEM((2, 17, PAIR, D), BF16),
             dma((2,)), dma((E,)), dma((E,)),
             dma((2, PIECES, 17)), dma((2, PIECES, 17)), dma((2, 17)), dma((2, 16)),
@@ -464,42 +474,39 @@
         compiler_params=pltpu.CompilerParams(
             collective_id=0, has_side_effects=True, vmem_limit_bytes=60 << 20
         ),
-    )(send, weight_in, weight_out)
-    back, grads = pl.pallas_call(
-        functools.partial(expert_kernel, factor),
-        out_shape=(rows_shape, shape((2, 8) + piece, BF16)),
+    )(expert_ids.T, gate_values.T, tokens, cotangent, weight_in, weight_out)
+    sums = (PIECES // 2,) + piece[1:]
+    returned, grads = pl.pallas_call(
+        functools.partial(scatter_kernel, factor),
+        out_shape=(rows_shape, shape(sums, F32)),
         in_specs=[VMEM] * 3,
-        out_specs=(VMEM, VMEM),
+        out_specs=(VMEM,) * 2,
         scratch_shapes=[
+            pltpu.VMEM(rows_shape.shape, BF16), pltpu.VMEM((2, 8) + piece, BF16),
             pltpu.VMEM((ROWS, D), BF16), pltpu.VMEM((ROWS, D), BF16),
+            pltpu.VMEM((D, ROWS), BF16), pltpu.VMEM((D, ROWS), BF16),
             pltpu.VMEM((ROWS, D), F32), pltpu.VMEM((ROWS, D), F32),
-        ],
-        compiler_params=big,
-    )(rows, full_in, full_out)
-    returned, grad_in, grad_out = pl.pallas_call(
-        scatter_kernel,
-        out_shape=(rows_shape, shape((64, FF // 2), F32), shape((64, FF // 2), F32)),
-        in_specs=[VMEM] * 2,
-        out_specs=(VMEM,) * 3,
-        scratch_shapes=[
             pltpu.VMEM((17,) + piece, BF16),
             pltpu.VMEM((16,) + piece, BF16), pltpu.VMEM((16,) + piece, BF16),
-            pltpu.VMEM((PIECES // 2,) + piece[1:], BF16),
+            pltpu.VMEM(sums, BF16),
             dma((E,)), dma((E,)), dma((PIECES, 16)), dma((PIECES, 17)),
             dma((PIECES, 16)), dma((PIECES, 16)), dma(()), dma(()),
         ],
         compiler_params=pltpu.CompilerParams(
             collective_id=1, has_side_effects=True, vmem_limit_bytes=60 << 20
         ),
-    )(back, grads)
-    layer_out, gate_grad, input_grad = pl.pallas_call(
+    )(rows, full_in, full_out)
+    layer_out, gate_grad, input_grad, grad_in, grad_out = pl.pallas_call(
         combine_kernel,
-        out_shape=(shape((TOK, D), BF16), shape((TOK, 2), F32), shape((TOK, D), BF16)),
-        in_specs=[VMEM] * 4,
-        out_specs=(VMEM,) * 3,
+        out_shape=(
+            shape((TOK, D), BF16), shape((2, TOK), F32), shape((TOK, D), BF16),
+            shape((64, FF // 2), F32), shape((64, FF // 2), F32),
+        ),
+        in_specs=[VMEM] * 5,
+        out_specs=(VMEM,) * 5,
         compiler_params=big,
-    )(returned, pos, gate_values, cotangent)
-    return layer_out, gate_grad, input_grad, grad_in, grad_out
+    )(returned, grads, pos, gate_values.T, cotangent)
+    return layer_out, gate_grad.T, input_grad, grad_in, grad_out
 
 
 def solution(mesh):

time: 241 us -> 221 us (0.917)
  Pallas kernels: 233 us -> 217 us
  local copies, waits for them, and re-layouts: 3.54 us -> 0 us
    pallas_call x4 -> x2, Pallas kernels: 132 us -> 116 us  [the longest x1 113 us: local(): pl.pallas_call(functools.partial(scatter_kernel, factor), out_shape=(rows...]
    unnamed x10 -> x0, local copies, waits for them, and re-layouts: 3.54 us -> none
where the time goes in v3:
time: 221 us; the launch traced here: 217 us
  Pallas kernels  217 us (98%)
    pallas_call x1, Pallas kernels, local(): pl.pallas_call(functools.partial(scatter_kernel, factor), out_shape=(rows...  113 us
    pallas_call x1, Pallas kernels, local(): pl.pallas_call(gather_kernel, out_shape=(rows_shape, shape((FF, D), BF16)...  100 us

profile of v3, /device:TPU:24, one launch (start us, length us, event | category | flops | bytes accessed | tf_op | source)
XLA Modules:
  0.0 217.4 jit_solution(17375292950048459028)
XLA Ops:
  0.6 100.4 %shard_map.101 = (bf16[32,18,8,128]{3,2,1,0:T(8,128)(2,1)}, bf16[1024,1024]{1,0:T(8,128)(2,1)}, bf16[1024,1024]{1,0:T(8,128)(2,1)}, s32[2,128]{1,0:T(2,128)}) custom-call(s32[2,128]{1,0:T(2,128)} %bitcast.5, f32[2,128]{1,0:T(2,128)} %bitcast.3, bf16[128,1024]{1,0:T(8,128)(2,1)} %tok_ref.1, bf16[128,1024]{1,0:T(8,128)(2,1)} %cot_ref.3, ...), custom_call_target="tpu_custom_call" | custom-call | tf_op jit(solution)/shard_map/pallas_call | solution.py:461
  101.0 113.2 %shard_map.102 = (bf16[32,18,8,128]{3,2,1,0:T(8,128)(2,1)}, f32[2,2,32,512]{3,2,1,0:T(8,128)}) custom-call(bf16[32,18,8,128]{3,2,1,0:T(8,128)(2,1)} %get-tuple-element.16.in_ref, bf16[1024,1024]{1,0:T(8,128)(2,1)} %get-tuple-element.17.fin_ref, bf16[1024,1024]{1,0:T(8,128)(2,1)} %get-tuple-element.18.fout_ref), custom_call_target="tpu_custom_call" | custom-call | tf_op jit(solution)/shard_map/pallas_call | solution.py:479
  214.2 3.2 %shard_map.103 = (bf16[128,1024]{1,0:T(8,128)(2,1)}, f32[2,128]{1,0:T(2,128)}, bf16[128,1024]{1,0:T(8,128)(2,1)}, f32[64,512]{1,0:T(8,128)}, f32[64,512]{1,0:T(8,128)}) custom-call(bf16[32,18,8,128]{3,2,1,0:T(8,128)(2,1)} %get-tuple-element.19.rows_ref, f32[2,2,32,512]{3,2,1,0:T(8,128)} %get-tuple-element.20.sum_ref, s32[2,128]{1,0:T(2,128)} %get-tuple-element.21.pos_ref, ...), custom_call_target="tpu_custom_call" | custom-call | tf_op jit(solution)/shard_map/pallas_call | solution.py:499
